TPU v7x, 256 devices: a whole 4x4x8 slice. The times are simulated.
256 devices in a mesh: docs: 8 (over x, core), seq: 32 (over z, y).
Axes of the slice: x: 4, y: 4, z: 8, core: 2. Of those that a mesh axis runs over, the one named last changes fastest.
Arguments:
- byte_input: bfloat16 [81920, 256], P(('docs', 'seq')), parts along dimension 0, may hold values from -6 to 6
- w_short: bfloat16 [1024, 1024], replicated, may hold values from -0.1875 to 0.1875
- w_attend: bfloat16 [1024, 3072], replicated, may hold values from -0.1875 to 0.1875
- w_expand: bfloat16 [1024, 1024], replicated, may hold values from -0.75 to 0.75
- out_grad: bfloat16 [81920, 256], P(('docs', 'seq')), parts along dimension 0, may hold values from -6 to 6
Outputs:
- byte_output: bfloat16 [81920, 256], P(('docs', 'seq')), parts along dimension 0
- input_grad: bfloat16 [81920, 256], P(('docs', 'seq')), parts along dimension 0
- grad_short: float32 [8192, 1024], P(('docs', 'seq')), parts along dimension 0
- grad_attend: float32 [8192, 3072], P(('docs', 'seq')), parts along dimension 0
- grad_expand: float32 [8192, 1024], P(('docs', 'seq')), parts along dimension 0
There are 8 independent parts, one for each index of `docs`. A program takes and returns all parts, laid end to end along the dimension named above; an argument that names none is the same for every part. Nothing has to cross between parts.
All inputs are finite; a program needn't handle non-finite values.
Results may differ from a plain program's by a relative error of at most 0.028.
Values may be sent and summed in bfloat16 or wider, within the bound.
No kernel may reach another device: no remote copies, remote signals or barrier semaphores. Data moves between devices by JAX's collectives and lax.ppermute only.
A program may use at most 128 MiB of HBM per device.

v0:
```python
import jax
import jax.numpy as jnp
from jax import lax
from jax.sharding import PartitionSpec as P

HEADS = 8
SCORE_BOUND = 16.0
EPSILON = 1e-06


def from_behind(value, axis, steps):
    count = lax.axis_size(axis)
    leading, last = (max(0, -steps), min(count, count - steps))
    return lax.ppermute(value, axis, [(source, source + steps) for source in range(leading, last)])


def rounded(value):
    return lax.optimization_barrier(value.astype(jnp.bfloat16))


def unit_heads(matrix):
    split = matrix.reshape(matrix.shape[0], HEADS, -1)
    scale = lax.rsqrt(jnp.mean(split * split, axis=2, keepdims=True) + EPSILON)
    return (split * scale, scale)


def norm_back(normed, scale, upstream):
    inner = jnp.mean(normed * upstream, axis=2, keepdims=True)
    return scale * (upstream - normed * inner)


def powers_of(query3, key3, query_pos, key_pos, factor):
    dots = jnp.einsum("thd,rhd->htr", query3, key3, preferred_element_type=jnp.float32)
    live = query_pos[:, None] >= key_pos[None, :]
    return jnp.where(live[None], jnp.exp(dots * factor), 0.0)


def local(byte_input, w_short, w_attend, w_expand, out_grad):
    shard_count = lax.axis_size("seq")
    own_index = lax.axis_index("seq")
    short_rows = byte_input.shape[0] // 4
    byte_width = byte_input.shape[1]
    attn_width = w_attend.shape[1] // 3
    head_size = attn_width // HEADS
    factor = SCORE_BOUND / head_size
    first_pos = own_index * short_rows
    query_pos = first_pos + jnp.arange(short_rows, dtype=jnp.int32)
    group_shards = min(8, shard_count)
    group_rows = group_shards * short_rows
    turns = own_index // group_shards + 1
    edge = from_behind(byte_input[-3:], "seq", 1)
    grouped = jnp.concatenate([edge, byte_input[:-3]], axis=0).reshape(short_rows, 4 * byte_width)
    hidden = jnp.dot(grouped, w_short, preferred_element_type=jnp.float32)
    hidden_scale = lax.rsqrt(jnp.mean(hidden * hidden, axis=1, keepdims=True) + EPSILON)
    normed = hidden * hidden_scale
    normed_b = normed.astype(jnp.bfloat16)
    projected = jnp.dot(normed_b, w_attend, preferred_element_type=jnp.float32)
    query_unit, query_scale = unit_heads(projected[:, :attn_width])
    key_unit, key_scale = unit_heads(projected[:, attn_width : 2 * attn_width])
    query3 = query_unit.astype(jnp.bfloat16)
    key_own = key_unit.astype(jnp.bfloat16).reshape(short_rows, attn_width)
    value_own = projected[:, 2 * attn_width :].astype(jnp.bfloat16)
    pair = jnp.concatenate([key_own, value_own], axis=1)

    def unpack(block):
        rows = block.shape[0]
        keys3 = block[:, :attn_width].reshape(rows, HEADS, head_size)
        values3 = block[:, attn_width:].reshape(rows, HEADS, head_size)
        return (keys3, values3)

    def absorb(totals, block, key_first):
        weighted, denom = totals
        keys3, values3 = unpack(block)
        key_pos = key_first + jnp.arange(block.shape[0], dtype=jnp.int32)
        powers = powers_of(query3, keys3, query_pos, key_pos, factor)
        weighted = weighted + jnp.einsum(
            "htr,rhd->thd", powers.astype(jnp.bfloat16), values3, preferred_element_type=jnp.float32
        )
        denom = denom + jnp.sum(powers, axis=2).T
        return (weighted, denom)

    zero_query = jnp.zeros((short_rows, HEADS, head_size), jnp.float32)
    zero_denom = jnp.zeros((short_rows, HEADS), jnp.float32)
    keep = lax.all_gather(pair, "seq", axis=0, tiled=True)

    def forward_step(block_no, totals):
        key_first = block_no * group_rows
        return absorb(totals, lax.dynamic_slice_in_dim(keep, key_first, group_rows, 0), key_first)

    weighted, denom = lax.fori_loop(0, turns, forward_step, (zero_query, zero_denom))
    attended = rounded((weighted / denom[:, :, None]).reshape(short_rows, attn_width))
    expanded = jnp.dot(attended, w_expand, preferred_element_type=jnp.float32)
    byte_output = (
        byte_input.astype(jnp.float32) + expanded.reshape(4 * short_rows, byte_width)
    ).astype(jnp.bfloat16)
    d_expand = out_grad.reshape(short_rows, 4 * byte_width)
    d_attended = rounded(jnp.dot(d_expand, w_expand.T, preferred_element_type=jnp.float32))
    d_attended = d_attended.astype(jnp.float32).reshape(short_rows, HEADS, head_size)
    inverse = 1.0 / denom
    grad3 = (d_attended * inverse[:, :, None]).astype(jnp.bfloat16)
    attended_f = attended.astype(jnp.float32).reshape(short_rows, HEADS, head_size)
    shifts = (jnp.sum(d_attended * attended_f, axis=2) * inverse).astype(jnp.bfloat16)
    shifts_cols = shifts.astype(jnp.float32).T[:, :, None]

    def score_grads(keys3, values3, key_first):
        key_pos = key_first + jnp.arange(keys3.shape[0], dtype=jnp.int32)
        powers = powers_of(query3, keys3, query_pos, key_pos, factor)
        grad_dot = jnp.einsum("thd,rhd->htr", grad3, values3, preferred_element_type=jnp.float32)
        d_score = (powers * (grad_dot - shifts_cols) * factor).astype(jnp.bfloat16)
        return (powers, d_score)

    def backward_step(block_no, totals):
        query_grad, term = totals
        key_first = block_no * group_rows
        keys3, values3 = unpack(lax.dynamic_slice_in_dim(keep, key_first, group_rows, 0))
        powers, d_score = score_grads(keys3, values3, key_first)
        query_grad = query_grad + jnp.einsum(
            "htr,rhd->thd", d_score, keys3, preferred_element_type=jnp.float32
        )
        key_part = jnp.einsum(
            "htr,thd->rhd", d_score, query3, preferred_element_type=jnp.float32
        ).reshape(group_rows, attn_width)
        value_part = jnp.einsum(
            "htr,thd->rhd", powers.astype(jnp.bfloat16), grad3, preferred_element_type=jnp.float32
        ).reshape(group_rows, attn_width)
        term = lax.dynamic_update_slice_in_dim(
            term, jnp.concatenate([key_part, value_part], axis=1), key_first, 0
        )
        return (query_grad, term)

    empty_term = jnp.zeros((shard_count * short_rows, 2 * attn_width), jnp.float32)
    query_grad, term = lax.fori_loop(0, turns, backward_step, (zero_query, empty_term))
    key_values = lax.psum_scatter(
        term.astype(jnp.bfloat16), "seq", scatter_dimension=0, tiled=True
    ).astype(jnp.float32)
    key_grad = key_values[:, :attn_width].reshape(short_rows, HEADS, head_size)
    value_grad = key_values[:, attn_width:].reshape(short_rows, HEADS, head_size)
    d_query = norm_back(query_unit, query_scale, query_grad).reshape(short_rows, attn_width)
    d_key = norm_back(key_unit, key_scale, key_grad).reshape(short_rows, attn_width)
    d_projected = jnp.concatenate(
        [d_query, d_key, value_grad.reshape(short_rows, attn_width)], axis=1
    ).astype(jnp.bfloat16)
    d_normed = jnp.dot(d_projected, w_attend.T, preferred_element_type=jnp.float32)
    d_hidden = (
        hidden_scale * (d_normed - normed * jnp.mean(normed * d_normed, axis=1, keepdims=True))
    ).astype(jnp.bfloat16)
    d_grouped = (
        jnp.dot(d_hidden, w_short.T, preferred_element_type=jnp.float32)
        .astype(jnp.bfloat16)
        .reshape(4 * short_rows, byte_width)
    )
    back_edge = from_behind(d_grouped[:3], "seq", -1)
    moved = jnp.concatenate([d_grouped[3:], back_edge], axis=0).astype(jnp.float32)
    input_grad = (out_grad.astype(jnp.float32) + moved).astype(jnp.bfloat16)

    def part(left, right):
        return jnp.dot(left.T, right, preferred_element_type=jnp.float32)

    grads = lax.psum_scatter(
        jnp.concatenate(
            [part(grouped, d_hidden), part(normed_b, d_projected), part(attended, d_expand)], axis=1
        ).astype(jnp.bfloat16),
        "seq",
        scatter_dimension=0,
        tiled=True,
    ).astype(jnp.float32)
    model_width = w_short.shape[1]
    grad_short = grads[:, :model_width]
    grad_attend = grads[:, model_width : model_width + 3 * attn_width]
    grad_expand = grads[:, model_width + 3 * attn_width :]
    return (byte_output, input_grad, grad_short, grad_attend, grad_expand)


def solution(mesh):
    in_specs = (P(("docs", "seq"), None), P(), P(), P(), P(("docs", "seq"), None))
    out_specs = (
        P(("docs", "seq"), None),
        P(("docs", "seq"), None),
        P(("docs", "seq"), None),
        P(("docs", "seq"), None),
        P(("docs", "seq"), None),
    )
    return jax.shard_map(local, mesh=mesh, in_specs=in_specs, out_specs=out_specs, check_vma=False)
```

profile of v0, /device:TPU:2, one launch (start us, length us, event | category | flops | bytes accessed | tf_op | source)
XLA Modules:
  0.0 731.4 jit_solution(5632253812423761780)
XLA Ops:
  8.1 3.5 collective-permute-start
  11.5 1.3 collective-permute-done
  14.5 4.1 fusion.21
  21.6 1.2 slice_bitcast_fusion.1
  23.7 1.0 reshape.175
  24.7 2.4 convolution_convert_fusion.4
  29.1 108.1 %all-gather.2.cloned.1.call-done = bf16[2560,2048]{1,0:T(8,128)(2,1)} async-done(((bf16[80,2048]{1,0:T(8,128)(2,1)}), bf16[2560,2048]{1,0:T(8,128)(2,1)}) %all-gather.2.cloned.1.call-update) | async-done | bytes 10485776 | tf_op jit(solution)/shard_map/all_gather | solution.py:84
  137.2 13.8 %copy.81 = bf16[2560,2048]{0,1:T(8,128)(2,1)} copy(bf16[2560,2048]{1,0:T(8,128)(2,1)} %all-gather.2.cloned.1.call-done) | data formatting | bytes 20971520
  151.0 3.5 while.26
  151.0 2.0 constant_dynamic-slice_fusion.3
  154.8 1.2 multiply_reduce_fusion.3
  156.2 5.2 broadcast_in_dim.51.clone
  161.4 14.7 %while.27 = (s32[]{:T(128)}, f32[80,8,128]{2,0,1:T(8,128)S(1)}, bf16[2560,2048]{1,0:T(8,128)(2,1)}, s32[]{:T(128)}, bf16[2560,2048]{0,1:T(8,128)(2,1)}, /*index=...) while((s32[]{:T(128)}, f32[80,8,128]{2,0,1:T(8,128)S(1)}, ...), condition=%wide.region_8.9_spmd.clone, body=%wide.region_7.8_spmd.clone.sunk | while | flops 532531936 | bytes 36319576 | solution.py:132
  161.4 1.9 fusion.93
  166.2 1.8 pad_maximum_fusion.8
  168.0 4.5 copy.135
  172.5 3.6 constant_dynamic-update-slice_fusion.2
  177.6 3.1 convolution_convert_fusion.1
  180.7 280.0 %reduce-scatter.3.cloned.1.call-done = bf16[80,2048]{1,0:T(8,128)(2,1)} async-done(((bf16[2560,2048]{1,0:T(8,128)(2,1)}), bf16[80,2048]{1,0:T(8,128)(2,1)}) %reduce-scatter.3.cloned.1.call-update) | async-done | bytes 327696 | tf_op jit(solution)/shard_map/reduce_scatter | solution.py:133
  460.7 1.0 convert_bitcast_fusion.2
  462.4 1.2 fusion.12
  463.6 4.9 multiply_reduce_fusion
  468.5 4.5 convolution_convert_fusion
  473.2 2.1 convolution_convert_fusion.2
  475.3 3.9 copy.91
  479.2 9.7 %pad_maximum_fusion.1 = bf16[1024,5120]{1,0:T(8,128)(2,1)} fusion(bf16[1024,1024]{1,0:T(8,128)(2,1)} %convolution_convert_fusion.1, bf16[1024,3072]{1,0:T(8,128)(2,1)} %convolution_convert_fusion, bf16[1024,1024]{1,0:T(8,128)(2,1)} %copy.91), kind=kLoop, calls=%fused_computation.25 | loop fusion | flops 31457280 | bytes 20971520 | tf_op jit(solution)/shard_map/concatenate | solution.py:160
  489.8 2.1 fusion.26
  492.9 1.3 collective-permute-start.1
  495.0 3.4 collective-permute-done.1
  499.1 222.5 %reduce-scatter.5.cloned.1.call-done = bf16[32,5120]{1,0:T(8,128)(2,1)} async-done(((bf16[1024,5120]{1,0:T(8,128)(2,1)}), bf16[32,5120]{1,0:T(8,128)(2,1)}) %reduce-scatter.5.cloned.1.call-update) | async-done | bytes 327696 | tf_op jit(solution)/shard_map/reduce_scatter | solution.py:159
  721.6 1.6 fusion.24
  723.2 1.7 slice.78
  (100 shorter events, 18.7 us)
Async XLA Ops:
  7.2 6.7 copy-start
  7.2 130.0 %all-gather.2.cloned.1.call-start = ((), (), s32[]{:S(2)}) async-start(), calls=%async_computation.2 | async-start | bytes 10813440 | tf_op jit(solution)/shard_map/all_gather | solution.py:84
  8.1 4.8 collective-permute-start
  13.9 4.7 copy-start.8
  18.6 1.0 copy-start.1
  19.6 3.2 copy-start.14
  19.7 0.7 copy-start.4
  20.9 0.7 copy-start.2
  23.6 437.1 %reduce-scatter.3.cloned.1.call-start = ((), (), s32[]{:S(2)}) async-start(), calls=%async_computation.3 | async-start | bytes 10813440 | tf_op jit(solution)/shard_map/reduce_scatter | solution.py:133
  24.7 4.0 copy-start.10
  154.6 1.4 copy-start.6
  154.6 1.4 copy-start.12
  176.1 545.5 %reduce-scatter.5.cloned.1.call-start = ((), (), s32[]{:S(2)}) async-start(), calls=%async_computation.4 | async-start | bytes 10813440 | tf_op jit(solution)/shard_map/reduce_scatter | solution.py:159
  177.6 284.2 %copy-start.5 = (f32[10,8,8,128]{3,2,1,0:T(8,128)S(1)}, f32[10,8,8,128]{3,2,1,0:T(8,128)}, u32[]{:S(2)}) copy-start(f32[10,8,8,128]{3,2,1,0:T(8,128)} %copy-done.4) | copy-start | bytes 983044
  177.6 284.8 %copy-start.3 = (f32[80,8,128]{2,1,0:T(8,128)S(1)}, f32[80,8,128]{2,1,0:T(8,128)}, u32[]{:S(2)}) copy-start(f32[80,8,128]{2,1,0:T(8,128)} %copy-done.2) | copy-start | bytes 983044
  180.7 282.9 %copy-start.11 = (bf16[80,1024]{1,0:T(8,128)(2,1)S(1)}, bf16[80,1024]{1,0:T(8,128)(2,1)}, u32[]{:S(2)}) copy-start(bf16[80,1024]{1,0:T(8,128)(2,1)} %copy_bitcast_fusion) | copy-start | bytes 491524
  468.5 4.6 copy-start.9
  488.9 0.9 copy-start.7
  491.9 2.3 copy-start.13
  491.9 6.5 copy-start.15
  492.9 5.5 collective-permute-start.1
Sparse Core Ops, SparseCore 0:
  23.7 113.4 all-gather.1
  176.2 284.4 reduce-scatter.2
  489.1 232.4 reduce-scatter.4
where the time goes:
time: 733 us; the launch traced here: 731 us
  waiting for transfers between devices  615 us (84%)
  local copies, waits for them, and re-layouts  45.6 us (6%)
  matrix products  28.5 us (4%)
  other arithmetic  22.7 us (3%)
  between operations  14.2 us (2%)
    reduce_scatter x1, waiting for transfers between devices, local(): lax.psum_scatter(term.astype(jnp.bfloat16), 'seq', scatter_dimension=0, t...  280 us
    reduce_scatter x1, waiting for transfers between devices, local(): lax.psum_scatter(jnp.concatenate([part(grouped, d_hidden), part(normed_b,...  222 us
    all_gather x1, waiting for transfers between devices, local(): keep = lax.all_gather(pair, 'seq', axis=0, tiled=True)  108 us
    unnamed x39, local copies, waits for them, and re-layouts  17.5 us
  transfers between devices with their start and end apart: 5, of which 5 were waited for; matrix products, arithmetic and copies ran while one was open for 2% of the time, Pallas kernels for 0%

commit v1 on v0

--- a/solution.py
+++ b/solution.py
@@ -6,6 +6,13 @@
 HEADS = 8
 SCORE_BOUND = 16.0
 EPSILON = 1e-06
+
+
+def swapped_in(block, name, dim):
+    n_dev = lax.axis_size(name)
+    blocks = jnp.stack([block for _ in range(n_dev)])
+    blocks = lax.all_to_all(blocks, name, split_axis=0, concat_axis=0)
+    return jnp.concatenate(blocks, axis=dim)
 
 
 def from_behind(value, axis, steps):
@@ -81,7 +88,7 @@
 
     zero_query = jnp.zeros((short_rows, HEADS, head_size), jnp.float32)
     zero_denom = jnp.zeros((short_rows, HEADS), jnp.float32)
-    keep = lax.all_gather(pair, "seq", axis=0, tiled=True)
+    keep = swapped_in(pair, "seq", 0)
 
     def forward_step(block_no, totals):
         key_first = block_no * group_rows

time: 733 us -> 879 us (1.20)
  waiting for transfers between devices: 615 us -> 744 us
  starting transfers between devices: 5.06 us -> 18.1 us
    all_to_all x0 -> x1, waiting for transfers between devices: none -> 226 us  [swapped_in(): blocks = lax.all_to_all(blocks, name, split_axis=0, concat_axis=0)]
    all_gather x1 -> x0, waiting for transfers between devices: 108 us -> none  [local(): keep = lax.all_gather(pair, 'seq', axis=0, tiled=True)]
    all_to_all x0 -> x1, starting transfers between devices: none -> 13.1 us  [swapped_in(): blocks = lax.all_to_all(blocks, name, split_axis=0, concat_axis=0)]
    reduce_scatter x1, waiting for transfers between devices: 280 us -> 291 us  [local(): lax.psum_scatter(term.astype(jnp.bfloat16), 'seq', scatter_dimension=0, t...]
where the time goes in v1:
time: 879 us; the launch traced here: 878 us
  waiting for transfers between devices  744 us (85%)
  local copies, waits for them, and re-layouts  50 us (6%)
  matrix products  28.5 us (3%)
  other arithmetic  21.9 us (2%)
  starting transfers between devices  18.1 us (2%)
  between operations  14.5 us (2%)
    reduce_scatter x1, waiting for transfers between devices, local(): lax.psum_scatter(term.astype(jnp.bfloat16), 'seq', scatter_dimension=0, t...  291 us
    all_to_all x1, waiting for transfers between devices, swapped_in(): blocks = lax.all_to_all(blocks, name, split_axis=0, concat_axis=0)  226 us
    reduce_scatter x1, waiting for transfers between devices, local(): lax.psum_scatter(jnp.concatenate([part(grouped, d_hidden), part(normed_b,...  223 us
  transfers between devices with their start and end apart: 5, of which 5 were waited for; matrix products, arithmetic and copies ran while one was open for 2% of the time, Pallas kernels for 0%

profile of v1, /device:TPU:2, one launch (start us, length us, event | category | flops | bytes accessed | tf_op | source)
XLA Modules:
  0.0 877.6 jit_solution(17153321744082066325)
XLA Ops:
  8.0 3.5 collective-permute-start
  11.5 1.3 collective-permute-done
  14.5 4.1 fusion.21
  21.6 1.2 slice_bitcast_fusion.1
  22.8 5.3 stack.2
  28.1 13.1 %all-to-all-start = ((bf16[32,80,2048]{2,1,0:T(8,128)(2,1)}), bf16[32,80,2048]{2,1,0:T(8,128)(2,1)}, u32[]{:S(2)}, u32[]{:S(2)}) async-start(bf16[32,80,2048]{2,1,0:T(8,128)(2,1)} %stack.2), calls=%async_computation | async-start | bytes 20971520 | tf_op jit(solution)/shard_map/all_to_all | solution.py:14
  41.4 2.4 convolution_convert_fusion.4
  45.9 226.2 %all-to-all-done = bf16[32,80,2048]{2,1,0:T(8,128)(2,1)} async-done(((bf16[32,80,2048]{2,1,0:T(8,128)(2,1)}), bf16[32,80,2048]{2,1,0:T(8,128)(2,1)}, u32[]{:S(2)}, u32[]{:S(2)}) %all-to-all-start) | async-done | bytes 10485792 | tf_op jit(solution)/shard_map/all_to_all | solution.py:14
  272.1 13.8 %copy.96 = bf16[2560,2048]{0,1:T(8,128)(2,1)} copy(bf16[2560,2048]{1,0:T(8,128)(2,1)} %bitcast) | data formatting | bytes 20971520
  285.9 3.5 while.26
  286.0 2.0 constant_dynamic-slice_fusion.3
  289.7 1.2 multiply_reduce_fusion.3
  291.1 5.2 broadcast_in_dim.51.clone
  296.3 14.7 %while.27 = (s32[]{:T(128)}, f32[80,8,128]{2,0,1:T(8,128)S(1)}, bf16[2560,2048]{1,0:T(8,128)(2,1)}, s32[]{:T(128)}, bf16[2560,2048]{0,1:T(8,128)(2,1)}, /*index=...) while((s32[]{:T(128)}, f32[80,8,128]{2,0,1:T(8,128)S(1)}, ...), condition=%wide.region_8.9_spmd.clone, body=%wide.region_7.8_spmd.clone.sunk | while | flops 532531936 | bytes 36319576 | solution.py:139
  296.3 1.9 fusion.93
  301.1 1.8 pad_maximum_fusion.8
  302.9 4.5 copy.150
  307.4 3.6 constant_dynamic-update-slice_fusion.2
  312.6 3.1 convolution_convert_fusion.1
  315.7 290.6 %reduce-scatter.3.cloned.1.call-done = bf16[80,2048]{1,0:T(8,128)(2,1)} async-done(((bf16[2560,2048]{1,0:T(8,128)(2,1)}), bf16[80,2048]{1,0:T(8,128)(2,1)}) %reduce-scatter.3.cloned.1.call-update) | async-done | bytes 327696 | tf_op jit(solution)/shard_map/reduce_scatter | solution.py:140
  608.0 1.2 fusion.12
  609.1 4.9 multiply_reduce_fusion
  614.1 4.5 convolution_convert_fusion
  618.7 2.1 convolution_convert_fusion.2
  620.8 3.9 copy.106
  624.7 9.7 %pad_maximum_fusion.1 = bf16[1024,5120]{1,0:T(8,128)(2,1)} fusion(bf16[1024,1024]{1,0:T(8,128)(2,1)} %convolution_convert_fusion.1, bf16[1024,3072]{1,0:T(8,128)(2,1)} %convolution_convert_fusion, bf16[1024,1024]{1,0:T(8,128)(2,1)} %copy.106), kind=kLoop, calls=%fused_computation.25 | loop fusion | flops 31457280 | bytes 20971520 | tf_op jit(solution)/shard_map/concatenate | solution.py:167
  635.4 2.1 fusion.26
  638.5 1.3 collective-permute-start.1
  640.5 3.4 collective-permute-done.1
  644.7 222.8 %reduce-scatter.5.cloned.1.call-done = bf16[32,5120]{1,0:T(8,128)(2,1)} async-done(((bf16[1024,5120]{1,0:T(8,128)(2,1)}), bf16[32,5120]{1,0:T(8,128)(2,1)}) %reduce-scatter.5.cloned.1.call-update) | async-done | bytes 327696 | tf_op jit(solution)/shard_map/reduce_scatter | solution.py:166
  867.4 1.6 fusion.24
  869.0 1.7 slice.78
  (102 shorter events, 19.1 us)
Async XLA Ops:
  7.2 6.7 copy-start
  8.0 4.8 collective-permute-start
  13.9 4.7 copy-start.8
  18.5 1.0 copy-start.1
  19.6 3.2 copy-start.14
  19.6 0.7 copy-start.4
  20.9 0.7 copy-start.2
  28.1 13.2 %copy-start.15 = (bf16[320,256]{1,0:T(8,128)(2,1)S(1)}, bf16[320,256]{1,0:T(8,128)(2,1)}, u32[]{:S(2)}) copy-start(bf16[320,256]{1,0:T(8,128)(2,1)} %param.13) | copy-start | bytes 491524
  28.1 244.0 %all-to-all-start = ((bf16[32,80,2048]{2,1,0:T(8,128)(2,1)}), bf16[32,80,2048]{2,1,0:T(8,128)(2,1)}, u32[]{:S(2)}, u32[]{:S(2)}) async-start(bf16[32,80,2048]{2,1,0:T(8,128)(2,1)} %stack.2), calls=%async_computation | async-start | bytes 20971520 | tf_op jit(solution)/shard_map/all_to_all | solution.py:14
  41.2 565.0 %reduce-scatter.3.cloned.1.call-start = ((), (), s32[]{:S(2)}) async-start(), calls=%async_computation.3 | async-start | bytes 10813440 | tf_op jit(solution)/shard_map/reduce_scatter | solution.py:140
  41.4 4.0 copy-start.10
  289.6 1.4 copy-start.6
  289.6 1.4 copy-start.12
  311.1 556.4 %reduce-scatter.5.cloned.1.call-start = ((), (), s32[]{:S(2)}) async-start(), calls=%async_computation.4 | async-start | bytes 10813440 | tf_op jit(solution)/shard_map/reduce_scatter | solution.py:166
  312.6 294.8 %copy-start.5 = (f32[10,8,8,128]{3,2,1,0:T(8,128)S(1)}, f32[10,8,8,128]{3,2,1,0:T(8,128)}, u32[]{:S(2)}) copy-start(f32[10,8,8,128]{3,2,1,0:T(8,128)} %copy-done.4) | copy-start | bytes 983044
  312.6 295.4 %copy-start.3 = (f32[80,8,128]{2,1,0:T(8,128)S(1)}, f32[80,8,128]{2,1,0:T(8,128)}, u32[]{:S(2)}) copy-start(f32[80,8,128]{2,1,0:T(8,128)} %copy-done.2) | copy-start | bytes 983044
  315.7 293.5 %copy-start.11 = (bf16[80,1024]{1,0:T(8,128)(2,1)S(1)}, bf16[80,1024]{1,0:T(8,128)(2,1)}, u32[]{:S(2)}) copy-start(bf16[80,1024]{1,0:T(8,128)(2,1)} %copy_bitcast_fusion) | copy-start | bytes 491524
  614.1 4.6 copy-start.9
  634.5 0.9 copy-start.7
  637.5 2.3 copy-start.13
  637.5 6.5 copy-start.16
  638.5 5.5 collective-permute-start.1
Sparse Core Ops, SparseCore 0:
  311.2 295.0 reduce-scatter.2
  634.6 232.7 reduce-scatter.4
